TPU v7x, 32 devices: a whole 2x2x4 slice. The times are simulated.
32 devices in a mesh: expert: 4 (over y, x), shard: 8 (over z, core).
Axes of the slice: x: 2, y: 2, z: 4, core: 2. Of those that a mesh axis runs over, the one named last changes fastest.
Arguments:
- hidden: bfloat16 [64, 4096], P('shard'), may hold values from -6 to 6
- queries: bfloat16 [64, 32, 128], P('shard', 'expert'), may hold values from -30 to 30
- key_cache: bfloat16 [64, 512, 8, 128], P('shard', None, 'expert'), may hold values from -16 to 16
- value_cache: bfloat16 [64, 512, 8, 128], P('shard', None, 'expert'), may hold values from -6 to 6
- out_weight: bfloat16 [4096, 4096], P('expert', 'shard'), may hold values from -0.09375 to 0.09375
- norm_gain: bfloat16 [4096], replicated, may hold values from 0.099609375 to 1.8984375
- router: bfloat16 [4096, 8], replicated, may hold values from -0.09375 to 0.09375
- expert_ids: int32 [64, 2], replicated, may hold values from 0 to 7, all different within a row; in each aligned block of 64 rows (0 to 63, 64 to 127, ...) at most 32 rows name the same one
- gate_weight: bfloat16 [8, 4096, 14336], P('expert', None, 'shard'), may hold values from -0.09375 to 0.09375
- up_weight: bfloat16 [8, 4096, 14336], P('expert', None, 'shard'), may hold values from -0.09375 to 0.09375
- down_weight: bfloat16 [8, 14336, 4096], P('expert', 'shard'), may hold values from -0.046875 to 0.046875
Outputs:
- layer_out: bfloat16 [64, 4096], P('shard')
Inputs may be any that keep to these rules, and one draw needn't show every extreme that they name: `expert_ids`: each token names two different experts; over all 64 tokens no expert is named by more than 32 tokens, a bound that some block reaches.
All inputs are finite; a program needn't handle non-finite values.
Results may differ from a plain program's by a relative error of at most 0.008.
Values may be sent and summed in bfloat16 or wider, within the bound.
A program may use at most 128 MiB of HBM per device.

v0:
```python
import math
import jax
import jax.numpy as jnp
from jax import lax
from jax.sharding import PartitionSpec as P


def on_device(
    hidden,
    queries,
    key_cache,
    value_cache,
    out_weight,
    norm_gain,
    router,
    expert_ids,
    gate_weight,
    up_weight,
    down_weight,
):
    count_local, heads_local, head_size = queries.shape
    kv_local = key_cache.shape[2]
    per_kv = heads_local // kv_local
    query_blocks = queries.reshape(count_local, kv_local, per_kv, head_size)
    scores = jnp.einsum(
        "tkgd,tpkd->tkgp", query_blocks, key_cache, preferred_element_type=jnp.float32
    ) / math.sqrt(head_size)
    attn_weights = jax.nn.softmax(scores, axis=-1).astype(jnp.bfloat16)
    attended = jnp.einsum(
        "tkgp,tpkd->tkgd", attn_weights, value_cache, preferred_element_type=jnp.float32
    )
    attended = attended.astype(jnp.bfloat16).reshape(count_local, heads_local * head_size)
    all_attended = lax.all_gather(attended, "shard", axis=0, tiled=True)
    partial_cols = jnp.dot(all_attended, out_weight, preferred_element_type=jnp.float32)
    partial_heads = lax.all_to_all(partial_cols, "shard", split_axis=0, concat_axis=1, tiled=True)
    attn_out = lax.psum(partial_heads, "expert")
    stream = hidden.astype(jnp.float32) + attn_out
    scaled = stream * lax.rsqrt(jnp.mean(stream * stream, axis=-1, keepdims=True) + 1e-05)
    normed = (scaled * norm_gain.astype(jnp.float32)).astype(jnp.bfloat16)
    everyone = lax.all_gather(normed, "shard", axis=0, tiled=True)
    token_count = everyone.shape[0]
    logits = jnp.dot(everyone, router, preferred_element_type=jnp.float32)
    top_first = jnp.take_along_axis(logits, expert_ids[:, 0:1], axis=1)[:, 0]
    top_second = jnp.take_along_axis(logits, expert_ids[:, 1:2], axis=1)[:, 0]
    weight_first = 1.0 / (1.0 + jnp.exp(top_second - top_first))
    weight_second = 1.0 / (1.0 + jnp.exp(top_first - top_second))
    local_experts = gate_weight.shape[0]
    group_index = lax.axis_index("expert")
    summed = jnp.zeros((token_count, everyone.shape[1]), jnp.float32)
    for member in range(local_experts):
        expert = group_index * local_experts + member
        in_first = expert_ids[:, 0] == expert
        in_second = expert_ids[:, 1] == expert
        routed_weight = jnp.where(in_first, weight_first, 0.0) + jnp.where(
            in_second, weight_second, 0.0
        )
        gated = jnp.dot(everyone, gate_weight[member], preferred_element_type=jnp.float32)
        upward = jnp.dot(everyone, up_weight[member], preferred_element_type=jnp.float32)
        activated = (jax.nn.silu(gated) * upward).astype(jnp.bfloat16)
        expert_out = jnp.dot(activated, down_weight[member], preferred_element_type=jnp.float32)
        summed = summed + routed_weight[:, None] * expert_out
    reduced = lax.psum_scatter(summed, "shard", scatter_dimension=0, tiled=True)
    expert_mix = lax.psum(reduced, "expert")
    return (stream + expert_mix).astype(jnp.bfloat16)


def solution(mesh):
    in_specs = (
        P("shard", None),
        P("shard", "expert", None),
        P("shard", None, "expert", None),
        P("shard", None, "expert", None),
        P("expert", "shard"),
        P(),
        P(),
        P(),
        P("expert", None, "shard"),
        P("expert", None, "shard"),
        P("expert", "shard", None),
    )
    out_specs = P("shard", None)
    return jax.shard_map(
        on_device, mesh=mesh, in_specs=in_specs, out_specs=out_specs, check_vma=False
    )
```

profile of v0, /device:TPU:0, one launch (start us, length us, event | category | flops | bytes accessed | tf_op | source)
XLA Modules:
  0.0 225.8 jit_solution(6295233523832174419)
XLA Ops:
  6.5 1.6 copy-done
  8.1 1.4 fusion.46
  9.7 2.0 fusion.49
  11.8 15.7 %all_gather.6 = bf16[64,1024]{1,0:T(8,128)(2,1)S(1)} all-gather(bf16[8,1024]{1,0:T(8,128)(2,1)S(1)} %reshape.37), channel_id=1, replica_groups=mesh['expert'=4,'shard'=8] {'shard'}, dimensions={0}, use_global_device_ids=true | all-gather | bytes 147456 | tf_op jit(solution)/shard_map/all_gather | solution.py:33
  27.5 2.2 convolution_bitcast_fusion
  29.7 4.6 %all-to-all-start = ((f32[8,8,512]{2,1,0:T(8,128)}), f32[8,8,512]{2,1,0:T(8,128)S(1)}, u32[]{:S(2)}, u32[]{:S(2)}) async-start(f32[8,8,512]{2,1,0:T(8,128)} %convolution_bitcast_fusion), calls=%async_computation | async-start | bytes 262144 | tf_op jit(solution)/shard_map/all_to_all | solution.py:35
  34.3 0.7 convert_element_type.27
  35.0 0.8 fusion.78
  35.8 5.2 %all-to-all-done = f32[8,8,512]{2,1,0:T(8,128)S(1)} async-done(((f32[8,8,512]{2,1,0:T(8,128)}), f32[8,8,512]{2,1,0:T(8,128)S(1)}, u32[]{:S(2)}, u32[]{:S(2)}) %all-to-all-start) | async-done | bytes 131104 | tf_op jit(solution)/shard_map/all_to_all | solution.py:35
  41.0 0.6 copy-done.4
  41.8 41.4 %all-reduce.3.cloned.1.call-done = f32[8,4096]{1,0:T(8,128)} async-done(((f32[8,4096]{1,0:T(8,128)}), f32[8,4096]{1,0:T(8,128)}) %all-reduce.3.cloned.1.call-update) | async-done | bytes 131088 | tf_op jit(solution)/shard_map/psum | solution.py:36
  83.2 1.1 multiply_reduce_fusion
  84.2 1.0 multiply_convert_fusion
  85.2 14.7 %all_gather.7 = bf16[64,4096]{1,0:T(8,128)(2,1)S(1)} all-gather(bf16[8,4096]{1,0:T(8,128)(2,1)S(1)} %multiply_convert_fusion), channel_id=1, replica_groups=mesh['expert'=4,'shard'=8] {'shard'}, dimensions={0}, use_global_device_ids=true | all-gather | bytes 589824 | tf_op jit(solution)/shard_map/all_gather | solution.py:40
  100.0 6.5 %fusion.5 = f32[64,1792]{1,0:T(8,128)S(1)} fusion(bf16[64,4096]{1,0:T(8,128)(2,1)S(1)} %all_gather.7, bf16[2,4096,1792]{2,1,0:T(8,128)(2,1)} %param.21), kind=kOutput, calls=%fused_computation.7 | convolution fusion | flops 939524096 | bytes 15663104 | tf_op jit(solution)/shard_map/dot_general | solution.py:57
  106.4 6.4 %fusion.11 = f32[64,1792]{1,0:T(8,128)S(1)} fusion(bf16[64,4096]{1,0:T(8,128)(2,1)S(1)} %all_gather.7, bf16[2,4096,1792]{2,1,0:T(8,128)(2,1)} %param.21), kind=kOutput, calls=%fused_computation.13 | convolution fusion | flops 939524096 | bytes 15663104 | tf_op jit(solution)/shard_map/dot_general | solution.py:57
  112.9 0.2 fusion.80
  113.2 0.7 gather_fusion
  113.9 0.7 gather_fusion.1
  114.7 13.1 %fusion.25 = f32[64,4096]{1,0:T(8,128)} fusion(bf16[2,1792,4096]{2,1,0:T(8,128)(2,1)} %param.23, bf16[64,4096]{1,0:T(8,128)(2,1)S(1)} %all_gather.7, bf16[2,4096,1792]{2,1,0:T(8,128)(2,1)} %param.22, f32[64]{0:T(128)S(1)} %fusion.73, f32[64,1792]{1,0:T(8,128)S(1)} %fusion.5), kind=kOutput, calls=%fused_computation.23 | convolution fusion | flops 1879998464 | bytes 31392000 | tf_op jit(solution)/shard_map/dot_general | solution.py:60
  127.8 13.6 %fusion.22 = f32[64,4096]{1,0:T(8,128)} fusion(f32[64,4096]{1,0:T(8,128)} %fusion.25, bf16[2,1792,4096]{2,1,0:T(8,128)(2,1)} %param.23, bf16[64,4096]{1,0:T(8,128)(2,1)S(1)} %all_gather.7, bf16[2,4096,1792]{2,1,0:T(8,128)(2,1)} %param.22, f32[64]{0:T(128)S(1)} %get-tuple-element.6, f32[64,1792]{1,0:T(8,128)S(1)} %fusion.11), kind=kOutput, calls=%fused_computation.22 | convolution fusion | flops 1880260608 | bytes 32440576 | tf_op jit(solution)/shard_map/dot_general | solution.py:60
  141.5 32.9 %reduce-scatter.2.cloned.1.call-done = f32[8,4096]{1,0:T(8,128)} async-done(((f32[64,4096]{1,0:T(8,128)}), f32[8,4096]{1,0:T(8,128)}) %reduce-scatter.2.cloned.1.call-update) | async-done | bytes 131088 | tf_op jit(solution)/shard_map/reduce_scatter | solution.py:62
  174.4 43.3 %all-reduce.5.cloned.1.call-done = f32[8,4096]{1,0:T(8,128)} async-done(((f32[8,4096]{1,0:T(8,128)}), f32[8,4096]{1,0:T(8,128)}) %all-reduce.5.cloned.1.call-update) | async-done | bytes 131088 | tf_op jit(solution)/shard_map/psum | solution.py:63
  217.7 1.6 add_convert_fusion
  (27 shorter events, 0.5 us)
Async XLA Ops:
  6.5 1.6 copy-start
  29.7 11.3 %all-to-all-start = ((f32[8,8,512]{2,1,0:T(8,128)}), f32[8,8,512]{2,1,0:T(8,128)S(1)}, u32[]{:S(2)}, u32[]{:S(2)}) async-start(f32[8,8,512]{2,1,0:T(8,128)} %convolution_bitcast_fusion), calls=%async_computation | async-start | bytes 262144 | tf_op jit(solution)/shard_map/all_to_all | solution.py:35
  34.3 48.9 %all-reduce.3.cloned.1.call-start = ((), (), s32[]{:S(2)}) async-start(), calls=%async_computation.2 | async-start | bytes 262144 | tf_op jit(solution)/shard_map/psum | solution.py:36
  41.0 0.6 copy-start.4
  41.7 132.7 %reduce-scatter.2.cloned.1.call-start = ((), (), s32[]{:S(2)}) async-start(), calls=%async_computation.3 | async-start | bytes 1179648 | tf_op jit(solution)/shard_map/reduce_scatter | solution.py:62
  100.0 12.9 %copy-start.5 = (bf16[4096,8]{0,1:T(8,128)(2,1)S(1)}, bf16[4096,8]{0,1:T(8,128)(2,1)}, u32[]{:S(2)}) copy-start(bf16[4096,8]{0,1:T(8,128)(2,1)} %param.19) | copy-start | bytes 196612
  100.0 14.7 %copy-start.6 = (s32[64,2]{0,1:T(2,128)S(1)}, s32[64,2]{0,1:T(2,128)}, u32[]{:S(2)}) copy-start(s32[64,2]{0,1:T(2,128)} %param.20) | copy-start | bytes 1540
  127.8 91.4 %copy-start.1 = (bf16[8,512,2,128]{3,2,1,0:T(2,128)(2,1)S(1)}, bf16[8,512,2,128]{3,2,1,0:T(2,128)(2,1)}, u32[]{:S(2)}) copy-start(bf16[8,512,2,128]{3,2,1,0:T(2,128)(2,1)} %param.15) | copy-start | bytes 6291460
  127.8 89.9 %copy-start.2 = (f32[8,4096]{1,0:T(8,128)S(1)}, f32[8,4096]{1,0:T(8,128)}, u32[]{:S(2)}) copy-start(f32[8,4096]{1,0:T(8,128)} %all-reduce.3.cloned.1.call-done) | copy-start | bytes 393220
  127.8 89.9 %copy-start.3 = (bf16[8,4096]{1,0:T(8,128)(2,1)S(1)}, bf16[8,4096]{1,0:T(8,128)(2,1)}, u32[]{:S(2)}) copy-start(bf16[8,4096]{1,0:T(8,128)(2,1)} %param.13) | copy-start | bytes 196612
  141.5 76.2 %all-reduce.5.cloned.1.call-start = ((), (), s32[]{:S(2)}) async-start(), calls=%async_computation.4 | async-start | bytes 262144 | tf_op jit(solution)/shard_map/psum | solution.py:63
Sparse Core Ops, SparseCore 0:
  41.8 41.2 all-reduce.2
  141.6 32.7 reduce-scatter.1
  177.3 40.3 all-reduce.4
where the time goes:
time: 226 us
  waiting for transfers between devices  123 us (54%)
  matrix products  45.5 us (20%)
  blocking collectives  30.5 us (13%)
  between operations  13.2 us (6%)
  other arithmetic  5.35 us (2%)
  starting transfers between devices  4.72 us (2%)
  local copies, waits for them, and re-layouts  3.76 us (2%)
    psum x1, waiting for transfers between devices, on_device(): expert_mix = lax.psum(reduced, 'expert')  43.3 us
    psum x1, waiting for transfers between devices, on_device(): attn_out = lax.psum(partial_heads, 'expert')  41.4 us
    reduce_scatter x1, waiting for transfers between devices, on_device(): reduced = lax.psum_scatter(summed, 'shard', scatter_dimension=0, tiled=True)  32.9 us
    dot_general x2, matrix products, on_device(): jnp.dot(activated, down_weight[member], preferred_element_type=jnp.float32)  26.7 us
    all_gather x1, blocking collectives, on_device(): all_attended = lax.all_gather(attended, 'shard', axis=0, tiled=True)  15.7 us
    all_gather x1, blocking collectives, on_device(): everyone = lax.all_gather(normed, 'shard', axis=0, tiled=True)  14.7 us
    dot_general x2, matrix products, on_device(): jnp.dot(everyone, gate_weight[member], preferred_element_type=jnp.float32)  12.9 us
    all_to_all x1, waiting for transfers between devices, on_device(): lax.all_to_all(partial_cols, 'shard', split_axis=0, concat_axis=1, tiled=...  5.22 us
  transfers between devices with their start and end apart: 4, of which 4 were waited for; matrix products, arithmetic and copies ran while one was open for 1% of the time, Pallas kernels for 0%

commit v1 on v0

--- a/solution.py
+++ b/solution.py
@@ -60,7 +60,7 @@
         expert_out = jnp.dot(activated, down_weight[member], preferred_element_type=jnp.float32)
         summed = summed + routed_weight[:, None] * expert_out
     reduced = lax.psum_scatter(summed, "shard", scatter_dimension=0, tiled=True)
-    expert_mix = lax.psum(reduced, "expert")
+    expert_mix = jnp.sum(lax.all_gather(reduced, "expert"), axis=0)
     return (stream + expert_mix).astype(jnp.bfloat16)
 
 

time: 226 us -> 193 us (0.85)
  waiting for transfers between devices: 123 us -> 79.5 us
  blocking collectives: 30.5 us -> 40.8 us
    psum x1 -> x0, waiting for transfers between devices: 43.3 us -> none  [on_device(): expert_mix = lax.psum(reduced, 'expert')]
    all_gather x0 -> x1, blocking collectives: none -> 10.3 us  [on_device(): expert_mix = jnp.sum(lax.all_gather(reduced, 'expert'), axis=0)]
  transfers between devices with their start and end apart: 4 -> 3, of which waited for: 4 -> 3; matrix products, arithmetic and copies ran while one was open for 1% -> 1% of each run, Pallas kernels for 0% -> 0%
where the time goes in v1:
time: 193 us; the launch traced here: 192 us
  waiting for transfers between devices  79.5 us (41%)
  matrix products  45.5 us (24%)
  blocking collectives  40.8 us (21%)
  between operations  13.5 us (7%)
  starting transfers between devices  4.68 us (2%)
  other arithmetic  4.48 us (2%)
  local copies, waits for them, and re-layouts  3.75 us (2%)
    psum x1, waiting for transfers between devices, on_device(): attn_out = lax.psum(partial_heads, 'expert')  41.4 us
    reduce_scatter x1, waiting for transfers between devices, on_device(): reduced = lax.psum_scatter(summed, 'shard', scatter_dimension=0, tiled=True)  32.9 us
    dot_general x2, matrix products, on_device(): jnp.dot(activated, down_weight[member], preferred_element_type=jnp.float32)  26.8 us
    all_gather x1, blocking collectives, on_device(): all_attended = lax.all_gather(attended, 'shard', axis=0, tiled=True)  15.7 us
    all_gather x1, blocking collectives, on_device(): everyone = lax.all_gather(normed, 'shard', axis=0, tiled=True)  14.7 us
    dot_general x2, matrix products, on_device(): jnp.dot(everyone, gate_weight[member], preferred_element_type=jnp.float32)  12.9 us
    all_gather x1, blocking collectives, on_device(): expert_mix = jnp.sum(lax.all_gather(reduced, 'expert'), axis=0)  10.3 us
    all_to_all x1, waiting for transfers between devices, on_device(): lax.all_to_all(partial_cols, 'shard', split_axis=0, concat_axis=1, tiled=...  5.22 us
  transfers between devices with their start and end apart: 3, of which 3 were waited for; matrix products, arithmetic and copies ran while one was open for 1% of the time, Pallas kernels for 0%

profile of v1, /device:TPU:0, one launch (start us, length us, event | category | flops | bytes accessed | tf_op | source)
XLA Modules:
  0.0 192.3 jit_solution(8444110503343114586)
XLA Ops:
  6.5 1.6 copy-done
  8.1 1.4 fusion.46
  9.7 2.0 %fusion.49 = bf16[8,2,4,128]{3,2,1,0:T(4,128)(2,1)S(1)} fusion(bf16[8,512,2,128]{3,2,1,0:T(2,128)(2,1)} %param.16, f32[8,2,4]{2,1,0:T(2,128)S(1)} %fusion.79, f32[8,2,4,512]{3,2,1,0:T(4,128)S(1)} %fusion.46), kind=kOutput, calls=%fused_computation.36 | convolution fusion | flops 8495679 | bytes 2244864 | tf_op jit(solution)/shard_map/tkgp,tpkd->tkgd/dot_general | solution.py:29
  11.8 15.7 %all_gather.12 = bf16[64,1024]{1,0:T(8,128)(2,1)S(1)} all-gather(bf16[8,1024]{1,0:T(8,128)(2,1)S(1)} %reshape.37), channel_id=1, replica_groups=mesh['expert'=4,'shard'=8] {'shard'}, dimensions={0}, use_global_device_ids=true | all-gather | bytes 147456 | tf_op jit(solution)/shard_map/all_gather | solution.py:33
  27.5 2.2 %convolution_bitcast_fusion = f32[8,8,512]{2,1,0:T(8,128)} fusion(bf16[64,1024]{1,0:T(8,128)(2,1)S(1)} %all_gather.12, bf16[1024,512]{1,0:T(8,128)(2,1)} %param.17), kind=kOutput, calls=%fused_computation.34 | convolution fusion | flops 67108864 | bytes 1310720 | tf_op jit(solution)/shard_map/dot_general | solution.py:34
  29.7 4.6 %all-to-all-start = ((f32[8,8,512]{2,1,0:T(8,128)}), f32[8,8,512]{2,1,0:T(8,128)S(1)}, u32[]{:S(2)}, u32[]{:S(2)}) async-start(f32[8,8,512]{2,1,0:T(8,128)} %convolution_bitcast_fusion), calls=%async_computation | async-start | bytes 262144 | tf_op jit(solution)/shard_map/all_to_all | solution.py:35
  34.3 0.7 convert_element_type.27
  35.0 0.8 fusion.78
  35.8 5.2 %all-to-all-done = f32[8,8,512]{2,1,0:T(8,128)S(1)} async-done(((f32[8,8,512]{2,1,0:T(8,128)}), f32[8,8,512]{2,1,0:T(8,128)S(1)}, u32[]{:S(2)}, u32[]{:S(2)}) %all-to-all-start) | async-done | bytes 131104 | tf_op jit(solution)/shard_map/all_to_all | solution.py:35
  41.0 0.6 copy-done.4
  41.8 41.4 %all-reduce.2.cloned.1.call-done = f32[8,4096]{1,0:T(8,128)} async-done(((f32[8,4096]{1,0:T(8,128)}), f32[8,4096]{1,0:T(8,128)}) %all-reduce.2.cloned.1.call-update) | async-done | bytes 131088 | tf_op jit(solution)/shard_map/psum | solution.py:36
  83.2 1.1 multiply_reduce_fusion
  84.2 1.0 multiply_convert_fusion
  85.2 14.7 %all_gather.13 = bf16[64,4096]{1,0:T(8,128)(2,1)S(1)} all-gather(bf16[8,4096]{1,0:T(8,128)(2,1)S(1)} %multiply_convert_fusion), channel_id=1, replica_groups=mesh['expert'=4,'shard'=8] {'shard'}, dimensions={0}, use_global_device_ids=true | all-gather | bytes 589824 | tf_op jit(solution)/shard_map/all_gather | solution.py:40
  100.0 6.5 %fusion.5 = f32[64,1792]{1,0:T(8,128)S(1)} fusion(bf16[64,4096]{1,0:T(8,128)(2,1)S(1)} %all_gather.13, bf16[2,4096,1792]{2,1,0:T(8,128)(2,1)} %param.21), kind=kOutput, calls=%fused_computation.7 | convolution fusion | flops 939524096 | bytes 15663104 | tf_op jit(solution)/shard_map/dot_general | solution.py:57
  106.4 6.4 %fusion.11 = f32[64,1792]{1,0:T(8,128)S(1)} fusion(bf16[64,4096]{1,0:T(8,128)(2,1)S(1)} %all_gather.13, bf16[2,4096,1792]{2,1,0:T(8,128)(2,1)} %param.21), kind=kOutput, calls=%fused_computation.13 | convolution fusion | flops 939524096 | bytes 15663104 | tf_op jit(solution)/shard_map/dot_general | solution.py:57
  112.9 0.2 fusion.80
  113.1 0.7 gather_fusion
  113.9 0.7 gather_fusion.1
  114.7 13.1 %fusion.25 = f32[64,4096]{1,0:T(8,128)} fusion(bf16[2,1792,4096]{2,1,0:T(8,128)(2,1)} %param.23, bf16[64,4096]{1,0:T(8,128)(2,1)S(1)} %all_gather.13, bf16[2,4096,1792]{2,1,0:T(8,128)(2,1)} %param.22, f32[64]{0:T(128)S(1)} %fusion.73, f32[64,1792]{1,0:T(8,128)S(1)} %fusion.5), kind=kOutput, calls=%fused_computation.23 | convolution fusion | flops 1879998464 | bytes 31392000 | tf_op jit(solution)/shard_map/dot_general | solution.py:60
  127.8 13.6 %fusion.22 = f32[64,4096]{1,0:T(8,128)} fusion(f32[64,4096]{1,0:T(8,128)} %fusion.25, bf16[2,1792,4096]{2,1,0:T(8,128)(2,1)} %param.23, bf16[64,4096]{1,0:T(8,128)(2,1)S(1)} %all_gather.13, bf16[2,4096,1792]{2,1,0:T(8,128)(2,1)} %param.22, f32[64]{0:T(128)S(1)} %get-tuple-element.6, f32[64,1792]{1,0:T(8,128)S(1)} %fusion.11), kind=kOutput, calls=%fused_computation.22 | convolution fusion | flops 1880260608 | bytes 32440576 | tf_op jit(solution)/shard_map/dot_general | solution.py:60
  141.5 32.9 %reduce-scatter.2.cloned.1.call-done = f32[8,4096]{1,0:T(8,128)} async-done(((f32[64,4096]{1,0:T(8,128)}), f32[8,4096]{1,0:T(8,128)}) %reduce-scatter.2.cloned.1.call-update) | async-done | bytes 131088 | tf_op jit(solution)/shard_map/reduce_scatter | solution.py:62
  174.4 10.3 %all-gather = f32[32,4096]{1,0:T(8,128)S(1)} all-gather(f32[8,4096]{1,0:T(8,128)} %reduce-scatter.2.cloned.1.call-done), channel_id=2, replica_groups=mesh['expert'=4,'shard'=8] {'expert'}, dimensions={0}, use_global_device_ids=true | all-gather | bytes 655360 | tf_op jit(solution)/shard_map/all_gather | solution.py:63
  184.8 0.7 add_convert_fusion
  (26 shorter events, 0.5 us)
Async XLA Ops:
  6.5 1.6 copy-start
  29.7 11.3 %all-to-all-start = ((f32[8,8,512]{2,1,0:T(8,128)}), f32[8,8,512]{2,1,0:T(8,128)S(1)}, u32[]{:S(2)}, u32[]{:S(2)}) async-start(f32[8,8,512]{2,1,0:T(8,128)} %convolution_bitcast_fusion), calls=%async_computation | async-start | bytes 262144 | tf_op jit(solution)/shard_map/all_to_all | solution.py:35
  34.3 48.9 %all-reduce.2.cloned.1.call-start = ((), (), s32[]{:S(2)}) async-start(), calls=%async_computation.2 | async-start | bytes 262144 | tf_op jit(solution)/shard_map/psum | solution.py:36
  41.0 0.6 copy-start.4
  41.7 132.7 %reduce-scatter.2.cloned.1.call-start = ((), (), s32[]{:S(2)}) async-start(), calls=%async_computation.3 | async-start | bytes 1179648 | tf_op jit(solution)/shard_map/reduce_scatter | solution.py:62
  100.0 12.9 %copy-start.5 = (bf16[4096,8]{0,1:T(8,128)(2,1)S(1)}, bf16[4096,8]{0,1:T(8,128)(2,1)}, u32[]{:S(2)}) copy-start(bf16[4096,8]{0,1:T(8,128)(2,1)} %param.19) | copy-start | bytes 196612
  100.0 14.7 %copy-start.6 = (s32[64,2]{0,1:T(2,128)S(1)}, s32[64,2]{0,1:T(2,128)}, u32[]{:S(2)}) copy-start(s32[64,2]{0,1:T(2,128)} %param.20) | copy-start | bytes 1540
  127.8 57.6 %copy-start.1 = (bf16[8,512,2,128]{3,2,1,0:T(2,128)(2,1)S(1)}, bf16[8,512,2,128]{3,2,1,0:T(2,128)(2,1)}, u32[]{:S(2)}) copy-start(bf16[8,512,2,128]{3,2,1,0:T(2,128)(2,1)} %param.15) | copy-start | bytes 6291460
  127.8 56.9 %copy-start.2 = (f32[8,4096]{1,0:T(8,128)S(1)}, f32[8,4096]{1,0:T(8,128)}, u32[]{:S(2)}) copy-start(f32[8,4096]{1,0:T(8,128)} %all-reduce.2.cloned.1.call-done) | copy-start | bytes 393220
  127.8 56.9 %copy-start.3 = (bf16[8,4096]{1,0:T(8,128)(2,1)S(1)}, bf16[8,4096]{1,0:T(8,128)(2,1)}, u32[]{:S(2)}) copy-start(bf16[8,4096]{1,0:T(8,128)(2,1)} %param.13) | copy-start | bytes 196612
Sparse Core Ops, SparseCore 0:
  41.8 41.2 all-reduce.1
  141.6 32.7 reduce-scatter.1
